TPU v7x, 32 devices: a whole 2x2x4 slice. The times are simulated.
32 devices in a mesh: space: 4 (over y, core), vel: 8 (over z, x).
Axes of the slice: x: 2, y: 2, z: 4, core: 2. Of those that a mesh axis runs over, the one named last changes fastest.
Arguments:
- distribution: float32 [64, 48, 2304], P('space', 'vel'), may hold values from 0 to 2
- collision_rate: float32 [64], P('space'), may hold values from 0.1 to 1
- face_flags: int32 [64], replicated, may hold values 0 or 1
Outputs:
- updated: float32 [64, 48, 2304], P('space', 'vel')
All inputs are finite; a program needn't handle non-finite values.
Results may differ from a plain program's by a relative error of at most 0.0001.
Values sent between devices are 32-bit elements; how exact they have to be, the bound alone decides.
A program may use at most 64 MiB of HBM per device.

v0:
```python
import math

import jax
import jax.numpy as jnp
from jax import lax
from jax.sharding import PartitionSpec as P

NV = 48


LENGTH = 8.0
RADIUS = 6.0
COURANT = 0.9
GOLDEN = (1.0 + math.sqrt(5.0)) / 2.0
DIRECTIONS = (
    (0.0, 1.0, GOLDEN),
    (0.0, -1.0, GOLDEN),
    (1.0, GOLDEN, 0.0),
    (-1.0, GOLDEN, 0.0),
    (GOLDEN, 0.0, 1.0),
    (-GOLDEN, 0.0, 1.0),
)
HIGHEST_MODE = lax.Precision.HIGHEST


def padded_2(cells, sides, width):
    for axis, dim in sides:
        count = lax.axis_size(axis)
        ends = count - 1
        head = lax.slice_in_dim(cells, 0, width, axis=dim)
        tail = lax.slice_in_dim(cells, cells.shape[dim] - width, cells.shape[dim], axis=dim)
        cells = jnp.concatenate(
            [
                lax.ppermute(tail, axis, [(i, (i + 1) % count) for i in range(ends)]),
                cells,
                lax.ppermute(head, axis, [((i + 1) % count, i) for i in range(ends)]),
            ],
            axis=dim,
        )
    return cells


def kernel_tables(points):
    index = jnp.arange(points, dtype=jnp.int32)
    wrapped = jnp.where(
        index < points // 2, index, jnp.where(index == points // 2, 0, index - points)
    )
    signed = wrapped.astype(jnp.float32) * (math.pi / LENGTH)
    wave_x = signed[:, None, None]
    wave_y = signed[None, :, None]
    wave_z = signed[None, None, :]
    square = wave_x * wave_x + wave_y * wave_y + wave_z * wave_z
    scale = math.sqrt(1.0 + GOLDEN * GOLDEN)
    gain_tables = []
    loss_tables = []
    for direction in DIRECTIONS:
        parallel = (wave_x * direction[0] + wave_y * direction[1] + wave_z * direction[2]) / scale
        across = jnp.sqrt(jnp.maximum(square - parallel * parallel, 0.0))
        gain_tables.append(jnp.cos(0.5 * RADIUS * parallel))
        loss_tables.append(jnp.sinc(RADIUS * across / (2.0 * math.pi)))
    loss_total = sum(loss_tables) / 6.0
    return (gain_tables, loss_tables, loss_total)


def dft_tables(points):
    index = jnp.arange(points, dtype=jnp.int32)
    product = index[:, None] * index[None, :] % points
    angle = product.astype(jnp.float32) * (2.0 * math.pi / points)
    cosine = jnp.cos(angle)
    sine = jnp.sin(angle)
    first_table = jnp.stack([cosine, -sine], axis=1)
    forward_table = jnp.stack(
        [jnp.stack([cosine, -sine], axis=1), jnp.stack([sine, cosine], axis=1)], axis=1
    )
    inverse_table = jnp.stack(
        [jnp.stack([cosine, sine], axis=1), jnp.stack([-sine, cosine], axis=1)], axis=1
    )
    return (first_table, forward_table, inverse_table)


def apply_table(tensor, table, dims):
    return lax.dot_general(
        tensor,
        table,
        ((dims, tuple(range(len(dims)))), ((), ())),
        precision=HIGHEST_MODE,
        preferred_element_type=jnp.float32,
    )


def forward_cube(cube, tables):
    first_table, forward_table, inverse_table = tables
    section_one = apply_table(cube, first_table, (1,))
    section_two = apply_table(section_one, forward_table, (1, 2))
    return apply_table(section_two, forward_table, (0, 2))


def inverse_pair(spectrum, tables):
    first_table, forward_table, inverse_table = tables
    points = spectrum.shape[0]
    section_one = apply_table(spectrum, inverse_table, (3, 2))
    section_two = apply_table(section_one, inverse_table, (0, 2))
    section_three = apply_table(section_two, inverse_table, (0, 2))
    section_three = section_three * (1.0 / float(points**3))
    return (section_three[:, :, 0, :], section_three[:, :, 1, :])


def packed(spectrum, first_factor, second_factor):
    real_part = spectrum[:, :, 0, :]
    imag_part = spectrum[:, :, 1, :]
    first_factor = jnp.asarray(first_factor, jnp.float32)
    first_factor = first_factor[:, :, :] if first_factor.ndim == 3 else first_factor
    joined_real = first_factor * real_part - second_factor * imag_part
    joined_imag = first_factor * imag_part + second_factor * real_part
    return jnp.stack([joined_real, joined_imag], axis=2)


def collide(spectrum, kernels, tables):
    gain_tables, loss_tables, loss_total = kernels
    products = []
    for gain_table, loss_table in zip(gain_tables, loss_tables):
        first_part, second_part = inverse_pair(packed(spectrum, gain_table, loss_table), tables)
        products.append(first_part * second_part)
    gain_total = sum(products) / 6.0
    cube, loss_field = inverse_pair(packed(spectrum, 1.0, loss_total), tables)
    return gain_total - cube * loss_field


def body(distribution, collision_rate, face_flags):
    cell_count, planes_dev, width = distribution.shape
    points = NV
    tables = dft_tables(points)
    kernels = kernel_tables(points)

    def from_cell(one_cell):
        cube = one_cell.reshape(points, points, points)
        spectrum = forward_cube(cube, tables)
        return collide(spectrum, kernels, tables).reshape(points, width)

    regrouped = lax.all_to_all(distribution, "vel", split_axis=0, concat_axis=1, tiled=True)
    cell_terms = lax.map(from_cell, regrouped)
    collision_term = lax.all_to_all(cell_terms, "vel", split_axis=1, concat_axis=0, tiled=True)
    offset = lax.axis_index("space") * cell_count
    padded = padded_2(distribution, (("space", 0),), 1)
    mirror = distribution.reshape(cell_count, planes_dev, points, points)[:, :, ::-1, :].reshape(
        cell_count, planes_dev, width
    )
    wall_flags = jnp.concatenate([face_flags, jnp.ones((1,), jnp.int32)])
    nearby_walls = lax.dynamic_slice_in_dim(wall_flags, offset, cell_count + 1)
    lower_wall = (nearby_walls[:-1] == 1)[:, None, None]
    upper_wall = (nearby_walls[1:] == 1)[:, None, None]
    at_start = (offset + jnp.arange(cell_count, dtype=jnp.int32) == 0)[:, None, None]
    lower_side = jnp.where(lower_wall, mirror, jnp.where(at_start, distribution, padded[:-2]))
    upper_side = jnp.where(upper_wall, mirror, padded[2:])
    column = (jnp.arange(width, dtype=jnp.int32) // points).astype(jnp.float32)
    centre = (points - 1) / 2.0
    speed = COURANT * (column - centre) / centre
    upwind_flux = jnp.where(
        speed > 0, speed * (distribution - lower_side), speed * (upper_side - distribution)
    )
    return distribution - upwind_flux + collision_rate[:, None, None] * collision_term


def solution(mesh):
    return jax.shard_map(
        body,
        mesh=mesh,
        in_specs=(P("space", "vel", None), P("space"), P()),
        out_specs=P("space", "vel", None),
        check_vma=False,
    )
```

profile of v0, /device:TPU:0, one launch (start us, length us, event | category | flops | bytes accessed | tf_op | source)
XLA Modules:
  0.0 419.0 jit_solution(5220611589307567298)
XLA Ops:
  2.8 7.3 %all-to-all-start = ((f32[16,6,2304]{2,1,0:T(8,128)}), f32[16,6,2304]{2,1,0:T(8,128)S(1)}, u32[]{:S(2)}, u32[]{:S(2)}) async-start(f32[16,6,2304]{2,1,0:T(8,128)} %copy.77), calls=%async_computation | async-start | bytes 2359296 | tf_op jit(solution)/shard_map/all_to_all | solution.py:140
  10.6 13.5 %add_multiply_fusion = (f32[48,48,48]{2,1,0:T(8,128)}, f32[48,48,48]{2,1,0:T(8,128)}, f32[48,48,48]{2,1,0:T(8,128)}, f32[48,48,48]{2,1,0:T(8,128)}, f32[48,48,48...) fusion(f32[48]{0:T(128)S(1)} %get-tuple-element.737, f32[48,48]{1,0:T(8,128)S(1)} %get-tuple-element.739, ...), kind=kLoop, calls=%fused_computation.329 | loop fusion | flops 26652672 | bytes 3161856 | tf_op jit(solution)/shard_map/div | solution.py:61
  24.2 14.4 %all-to-all-done = f32[16,6,2304]{2,1,0:T(8,128)S(1)} async-done(((f32[16,6,2304]{2,1,0:T(8,128)}), f32[16,6,2304]{2,1,0:T(8,128)S(1)}, u32[]{:S(2)}, u32[]{:S(2)}) %all-to-all-start) | async-done | bytes 884768 | tf_op jit(solution)/shard_map/all_to_all | solution.py:140
  39.3 347.2 %while.13 = (s32[]{:T(128)}, f32[2,48,2304]{2,0,1:T(2,128)}, f32[2,48,2304]{2,0,1:T(2,128)S(1)}, f32[48,2,48]{2,0,1:T(8,128)S(1)}, f32[48,2,2,48]{3,0,1,2:T(8,12...) while((s32[]{:T(128)}, f32[2,48,2304]{2,0,1:T(2,128)}, ...), condition=%wide.region_1.3_spmd.clone.clone.clone, body=%wide.region_0.2_spmd.clone.clone.clone.sunk | while | flops 5998288896 | bytes 128030208 | solution.py:141
  45.1 3.8 copy.170
  48.9 6.0 %fusion.365 = f32[48,48,2,48,1]{0,3,4,2,1:T(8,128)S(1)} fusion(f32[48,48,2,48,1]{1,0,2,4,3:T(8,128)} %copy.170, f32[48,2,2,48]{3,0,1,2:T(8,128)S(1)} %get-tuple-element.770), kind=kOutput, calls=%fused_computation.156.clone.1 | convolution fusion | flops 254803968 | bytes 1806336 | tf_op jit(solution)/shard_map/while/body/eval_jaxpr/dot_general | solution.py:82
  57.0 10.0 %fusion.367 = (f32[48,48,1,48]{3,1,2,0:T(8,128)}, f32[48,48,1,48]{3,1,2,0:T(8,128)}, f32[48,48,1,48]{3,1,2,0:T(8,128)S(1)}, f32[48,48,1,48]{3,1,2,0:T(8,128)S(1)...) fusion(f32[48,48,48]{2,1,0:T(8,128)S(1)} %copy-done.16, f32[48]{0:T(128)S(1)} %get-tuple-element.779, ...), kind=kLoop, calls=%fused_computation.117.clone.1 | loop fusion | flops 2211840 | bytes 4884672 | tf_op jit(solution)/shard_map/while/body/eval_jaxpr/sub | solution.py:113
  67.0 3.5 fusion.380
  70.5 4.3 %copy.176 = f32[48,48,2,48,1]{0,1,2,4,3:T(8,128)} copy(f32[48,48,2,48,1]{3,1,2,0,4:T(8,128)} %fusion.380) | data formatting | bytes 1769472 | tf_op jit(solution)/shard_map/while/body/eval_jaxpr/dot_general | solution.py:82
  74.8 6.0 %fusion.381 = f32[48,48,2,48,1]{0,3,4,2,1:T(8,128)S(1)} fusion(f32[48,48,2,48,1]{0,1,2,4,3:T(8,128)} %copy.176, f32[48,2,2,48]{3,0,1,2:T(8,128)S(1)} %get-tuple-element.772), kind=kOutput, calls=%fused_computation.148.clone.1 | convolution fusion | flops 254803968 | bytes 1806336 | tf_op jit(solution)/shard_map/while/body/eval_jaxpr/dot_general | solution.py:82
  80.8 3.5 bitcast_multiply_fusion.45
  84.3 3.5 fusion.382
  87.8 3.8 copy.177
  91.7 6.0 %fusion.383 = f32[48,48,2,48,1]{0,3,4,2,1:T(8,128)S(1)} fusion(f32[48,48,2,48,1]{0,1,2,4,3:T(8,128)} %copy.177, f32[48,2,2,48]{3,0,1,2:T(8,128)S(1)} %get-tuple-element.772), kind=kOutput, calls=%fused_computation.152.clone.1 | convolution fusion | flops 254803968 | bytes 1806336 | tf_op jit(solution)/shard_map/while/body/eval_jaxpr/dot_general | solution.py:82
  97.7 3.5 bitcast_multiply_fusion.46
  101.2 9.6 %fusion.370 = (f32[48,48,1,48]{3,1,2,0:T(8,128)}, f32[48,48,1,48]{3,1,2,0:T(8,128)}, f32[48,48,1,48]{3,1,2,0:T(8,128)S(1)}, f32[48,48,1,48]{3,1,2,0:T(8,128)S(1)}) fusion(f32[48,48,48]{2,1,0:T(8,128)S(1)} %copy-done.18, f32[48]{0:T(128)S(1)} %get-tuple-element.785, f32[48,48]{1,0:T(8,128)S(1)} %copy-done.24, f32[48,48,2,48]{3,1,2,0:T(8,128)S(1)} %fusion.366, ...), kind=kLoop, calls=%fused_computation.93.clone.1 | loop fusion | flops 1769472 | bytes 3557568 | tf_op jit(solution)/shard_map/while/body/eval_jaxpr/sub | solution.py:113
  114.3 3.9 copy.172
  118.2 6.0 %fusion.372 = f32[48,48,2,48,1]{0,3,4,2,1:T(8,128)S(1)} fusion(f32[48,48,2,48,1]{0,1,2,4,3:T(8,128)} %copy.172, f32[48,2,2,48]{3,0,1,2:T(8,128)S(1)} %get-tuple-element.772), kind=kOutput, calls=%fused_computation.132.clone.1 | convolution fusion | flops 254803968 | bytes 1806336 | tf_op jit(solution)/shard_map/while/body/eval_jaxpr/dot_general | solution.py:82
  124.3 3.5 bitcast_multiply_fusion.41
  127.7 3.5 fusion.373
  131.3 3.9 copy.173
  135.2 6.0 %fusion.374 = f32[48,48,2,48,1]{0,3,4,2,1:T(8,128)S(1)} fusion(f32[48,48,2,48,1]{0,1,2,4,3:T(8,128)} %copy.173, f32[48,2,2,48]{3,0,1,2:T(8,128)S(1)} %get-tuple-element.772), kind=kOutput, calls=%fused_computation.136.clone.1 | convolution fusion | flops 254803968 | bytes 1806336 | tf_op jit(solution)/shard_map/while/body/eval_jaxpr/dot_general | solution.py:82
  141.2 3.5 bitcast_multiply_fusion.42
  144.8 9.6 %fusion.375 = (f32[48,48,1,48]{3,1,2,0:T(8,128)}, f32[48,48,1,48]{3,1,2,0:T(8,128)}, f32[48,48,1,48]{3,1,2,0:T(8,128)S(1)}, f32[48,48,1,48]{3,1,2,0:T(8,128)S(1)}) fusion(f32[48,48,48]{2,1,0:T(8,128)S(1)} %copy-done.14, f32[48]{0:T(128)S(1)} %get-tuple-element.782, f32[48,48]{1,0:T(8,128)S(1)} %copy-done.26, f32[48,48,2,48]{3,1,2,0:T(8,128)S(1)} %fusion.366, ...), kind=kLoop, calls=%fused_computation.105.clone.1 | loop fusion | flops 1769472 | bytes 3557568 | tf_op jit(solution)/shard_map/while/body/eval_jaxpr/sub | solution.py:113
  159.5 6.0 %fusion.377 = f32[48,48,2,48,1]{0,3,4,2,1:T(8,128)S(1)} fusion(f32[48,48,2,48,1]{0,1,2,4,3:T(8,128)} %copy.174, f32[48,2,2,48]{3,0,1,2:T(8,128)S(1)} %get-tuple-element.772), kind=kOutput, calls=%fused_computation.140.clone.1 | convolution fusion | flops 254803968 | bytes 1806336 | tf_op jit(solution)/shard_map/while/body/eval_jaxpr/dot_general | solution.py:82
  167.6 3.5 fusion.378
  171.1 3.9 copy.175
  175.0 6.0 %fusion.379 = f32[48,48,2,48,1]{0,3,4,2,1:T(8,128)S(1)} fusion(f32[48,48,2,48,1]{0,1,2,4,3:T(8,128)} %copy.175, f32[48,2,2,48]{3,0,1,2:T(8,128)S(1)} %get-tuple-element.772), kind=kOutput, calls=%fused_computation.144.clone.1 | convolution fusion | flops 254803968 | bytes 1806336 | tf_op jit(solution)/shard_map/while/body/eval_jaxpr/dot_general | solution.py:82
  181.0 3.5 bitcast_multiply_fusion.44
  184.5 3.5 fusion.368
  188.0 3.9 copy.171
  191.9 6.2 %fusion.369 = f32[48,48,2,48,1]{0,3,4,2,1:T(8,128)S(1)} fusion(f32[48,48,2,48,1]{0,1,2,4,3:T(8,128)} %copy.171, f32[48,2,2,48]{3,0,1,2:T(8,128)S(1)} %get-tuple-element.772), kind=kOutput, calls=%fused_computation.128.clone.1 | convolution fusion | flops 254803968 | bytes 1806336 | tf_op jit(solution)/shard_map/while/body/eval_jaxpr/dot_general | solution.py:82
  200.5 4.2 fusion.384
  216.8 3.9 copy.170
  220.7 6.0 %fusion.365 = f32[48,48,2,48,1]{0,3,4,2,1:T(8,128)S(1)} fusion(f32[48,48,2,48,1]{1,0,2,4,3:T(8,128)} %copy.170, f32[48,2,2,48]{3,0,1,2:T(8,128)S(1)} %get-tuple-element.770), kind=kOutput, calls=%fused_computation.156.clone.1 | convolution fusion | flops 254803968 | bytes 1806336 | tf_op jit(solution)/shard_map/while/body/eval_jaxpr/dot_general | solution.py:82
  228.9 10.0 %fusion.367 = (f32[48,48,1,48]{3,1,2,0:T(8,128)}, f32[48,48,1,48]{3,1,2,0:T(8,128)}, f32[48,48,1,48]{3,1,2,0:T(8,128)S(1)}, f32[48,48,1,48]{3,1,2,0:T(8,128)S(1)...) fusion(f32[48,48,48]{2,1,0:T(8,128)S(1)} %copy-done.16, f32[48]{0:T(128)S(1)} %get-tuple-element.779, ...), kind=kLoop, calls=%fused_computation.117.clone.1 | loop fusion | flops 2211840 | bytes 4884672 | tf_op jit(solution)/shard_map/while/body/eval_jaxpr/sub | solution.py:113
  238.8 3.5 fusion.380
  242.3 3.9 copy.176
  246.2 6.0 %fusion.381 = f32[48,48,2,48,1]{0,3,4,2,1:T(8,128)S(1)} fusion(f32[48,48,2,48,1]{0,1,2,4,3:T(8,128)} %copy.176, f32[48,2,2,48]{3,0,1,2:T(8,128)S(1)} %get-tuple-element.772), kind=kOutput, calls=%fused_computation.148.clone.1 | convolution fusion | flops 254803968 | bytes 1806336 | tf_op jit(solution)/shard_map/while/body/eval_jaxpr/dot_general | solution.py:82
  252.3 3.5 bitcast_multiply_fusion.45
  255.7 3.5 fusion.382
  259.3 3.9 copy.177
  263.2 6.0 %fusion.383 = f32[48,48,2,48,1]{0,3,4,2,1:T(8,128)S(1)} fusion(f32[48,48,2,48,1]{0,1,2,4,3:T(8,128)} %copy.177, f32[48,2,2,48]{3,0,1,2:T(8,128)S(1)} %get-tuple-element.772), kind=kOutput, calls=%fused_computation.152.clone.1 | convolution fusion | flops 254803968 | bytes 1806336 | tf_op jit(solution)/shard_map/while/body/eval_jaxpr/dot_general | solution.py:82
  269.2 3.5 bitcast_multiply_fusion.46
  272.7 9.6 %fusion.370 = (f32[48,48,1,48]{3,1,2,0:T(8,128)}, f32[48,48,1,48]{3,1,2,0:T(8,128)}, f32[48,48,1,48]{3,1,2,0:T(8,128)S(1)}, f32[48,48,1,48]{3,1,2,0:T(8,128)S(1)}) fusion(f32[48,48,48]{2,1,0:T(8,128)S(1)} %copy-done.18, f32[48]{0:T(128)S(1)} %get-tuple-element.785, f32[48,48]{1,0:T(8,128)S(1)} %copy-done.24, f32[48,48,2,48]{3,1,2,0:T(8,128)S(1)} %fusion.366, ...), kind=kLoop, calls=%fused_computation.93.clone.1 | loop fusion | flops 1769472 | bytes 3557568 | tf_op jit(solution)/shard_map/while/body/eval_jaxpr/sub | solution.py:113
  285.8 4.0 copy.172
  289.8 6.0 %fusion.372 = f32[48,48,2,48,1]{0,3,4,2,1:T(8,128)S(1)} fusion(f32[48,48,2,48,1]{0,1,2,4,3:T(8,128)} %copy.172, f32[48,2,2,48]{3,0,1,2:T(8,128)S(1)} %get-tuple-element.772), kind=kOutput, calls=%fused_computation.132.clone.1 | convolution fusion | flops 254803968 | bytes 1806336 | tf_op jit(solution)/shard_map/while/body/eval_jaxpr/dot_general | solution.py:82
  299.3 3.5 fusion.373
  302.8 4.1 copy.173
  306.9 6.0 %fusion.374 = f32[48,48,2,48,1]{0,3,4,2,1:T(8,128)S(1)} fusion(f32[48,48,2,48,1]{0,1,2,4,3:T(8,128)} %copy.173, f32[48,2,2,48]{3,0,1,2:T(8,128)S(1)} %get-tuple-element.772), kind=kOutput, calls=%fused_computation.136.clone.1 | convolution fusion | flops 254803968 | bytes 1806336 | tf_op jit(solution)/shard_map/while/body/eval_jaxpr/dot_general | solution.py:82
  313.0 3.5 bitcast_multiply_fusion.42
  316.6 9.6 %fusion.375 = (f32[48,48,1,48]{3,1,2,0:T(8,128)}, f32[48,48,1,48]{3,1,2,0:T(8,128)}, f32[48,48,1,48]{3,1,2,0:T(8,128)S(1)}, f32[48,48,1,48]{3,1,2,0:T(8,128)S(1)}) fusion(f32[48,48,48]{2,1,0:T(8,128)S(1)} %copy-done.14, f32[48]{0:T(128)S(1)} %get-tuple-element.782, f32[48,48]{1,0:T(8,128)S(1)} %copy-done.26, f32[48,48,2,48]{3,1,2,0:T(8,128)S(1)} %fusion.366, ...), kind=kLoop, calls=%fused_computation.105.clone.1 | loop fusion | flops 1769472 | bytes 3557568 | tf_op jit(solution)/shard_map/while/body/eval_jaxpr/sub | solution.py:113
  331.0 6.0 %fusion.377 = f32[48,48,2,48,1]{0,3,4,2,1:T(8,128)S(1)} fusion(f32[48,48,2,48,1]{0,1,2,4,3:T(8,128)} %copy.174, f32[48,2,2,48]{3,0,1,2:T(8,128)S(1)} %get-tuple-element.772), kind=kOutput, calls=%fused_computation.140.clone.1 | convolution fusion | flops 254803968 | bytes 1806336 | tf_op jit(solution)/shard_map/while/body/eval_jaxpr/dot_general | solution.py:82
  339.1 3.5 fusion.378
  342.6 3.9 copy.175
  346.5 6.0 %fusion.379 = f32[48,48,2,48,1]{0,3,4,2,1:T(8,128)S(1)} fusion(f32[48,48,2,48,1]{0,1,2,4,3:T(8,128)} %copy.175, f32[48,2,2,48]{3,0,1,2:T(8,128)S(1)} %get-tuple-element.772), kind=kOutput, calls=%fused_computation.144.clone.1 | convolution fusion | flops 254803968 | bytes 1806336 | tf_op jit(solution)/shard_map/while/body/eval_jaxpr/dot_general | solution.py:82
  352.5 3.5 bitcast_multiply_fusion.44
  356.0 3.5 fusion.368
  359.5 3.9 copy.171
  363.5 6.2 %fusion.369 = f32[48,48,2,48,1]{0,3,4,2,1:T(8,128)S(1)} fusion(f32[48,48,2,48,1]{0,1,2,4,3:T(8,128)} %copy.171, f32[48,2,2,48]{3,0,1,2:T(8,128)S(1)} %get-tuple-element.772), kind=kOutput, calls=%fused_computation.128.clone.1 | convolution fusion | flops 254803968 | bytes 1806336 | tf_op jit(solution)/shard_map/while/body/eval_jaxpr/dot_general | solution.py:82
  372.0 4.2 fusion.384
  386.5 4.4 %all-to-all-start.1 = ((f32[2,48,2304]{2,0,1:T(2,128)}), f32[2,48,2304]{2,0,1:T(2,128)}, u32[]{:S(2)}, u32[]{:S(2)}) async-start(f32[2,48,2304]{2,0,1:T(2,128)} %get-tuple-element.142), calls=%async_computation.1 | async-start | bytes 1769472 | tf_op jit(solution)/shard_map/all_to_all | solution.py:142
  396.8 3.5 rev.3
  402.2 10.9 %all-to-all-done.1 = f32[2,48,2304]{2,0,1:T(2,128)} async-done(((f32[2,48,2304]{2,0,1:T(2,128)}), f32[2,48,2304]{2,0,1:T(2,128)}, u32[]{:S(2)}, u32[]{:S(2)}) %all-to-all-start.1) | async-done | bytes 884768 | tf_op jit(solution)/shard_map/all_to_all | solution.py:142
  (174 shorter events, 74.2 us)
Async XLA Ops:
  2.8 35.8 %all-to-all-start = ((f32[16,6,2304]{2,1,0:T(8,128)}), f32[16,6,2304]{2,1,0:T(8,128)S(1)}, u32[]{:S(2)}, u32[]{:S(2)}) async-start(f32[16,6,2304]{2,1,0:T(8,128)} %copy.77), calls=%async_computation | async-start | bytes 2359296 | tf_op jit(solution)/shard_map/all_to_all | solution.py:140
  10.0 14.1 %copy-start.31 = (f32[48]{0:T(128)}, f32[48]{0:T(128)S(1)}, u32[]{:S(2)}) copy-start(f32[48]{0:T(128)S(1)} %get-tuple-element.734) | copy-start | bytes 580
  10.6 13.6 %copy-start.21 = (f32[48,48]{1,0:T(8,128)}, f32[48,48]{1,0:T(8,128)S(1)}, u32[]{:S(2)}) copy-start(f32[48,48]{1,0:T(8,128)S(1)} %get-tuple-element.736) | copy-start | bytes 27652
  10.6 13.6 %copy-start.23 = (f32[48,48]{1,0:T(8,128)}, f32[48,48]{1,0:T(8,128)S(1)}, u32[]{:S(2)}) copy-start(f32[48,48]{1,0:T(8,128)S(1)} %get-tuple-element.738) | copy-start | bytes 27652
  10.6 13.6 %copy-start.25 = (f32[48,48]{1,0:T(8,128)}, f32[48,48]{1,0:T(8,128)S(1)}, u32[]{:S(2)}) copy-start(f32[48,48]{1,0:T(8,128)S(1)} %get-tuple-element.735) | copy-start | bytes 27652
  10.6 13.6 %copy-start.27 = (f32[48,48]{1,0:T(8,128)}, f32[48,48]{1,0:T(8,128)S(1)}, u32[]{:S(2)}) copy-start(f32[48,48]{1,0:T(8,128)S(1)} %get-tuple-element.732) | copy-start | bytes 27652
  38.6 0.7 copy-start.32
  54.9 2.1 copy-start.12
  54.9 2.1 copy-start.15
  54.9 2.1 copy-start.16
  54.9 2.1 copy-start.28
  80.8 3.5 copy-start.6
  80.8 3.5 copy-start.7
  97.7 3.6 copy-start.17
  97.7 3.5 copy-start.18
  97.7 3.5 copy-start.24
  124.2 3.5 copy-start.10
  124.2 3.5 copy-start.11
  141.2 3.6 copy-start.13
  141.2 3.6 copy-start.14
  141.2 3.6 copy-start.22
  141.2 3.6 copy-start.26
  165.5 2.1 copy-start.8
  165.6 2.1 copy-start.9
  181.0 3.5 copy-start.4
  181.0 3.5 copy-start.5
  191.9 8.3 %copy-start.2 = (f32[48,48,2,48]{3,1,2,0:T(8,128)S(1)}, f32[48,48,2,48]{3,1,2,0:T(8,128)}, u32[]{:S(2)}) copy-start(f32[48,48,2,48]{3,1,2,0:T(8,128)} %bitcast_multiply_fusion.41) | copy-start | bytes 2654212 | tf_op jit(solution)/shard_map/while
  191.9 8.3 %copy-start.3 = (f32[48,48,2,48]{3,1,2,0:T(8,128)S(1)}, f32[48,48,2,48]{3,1,2,0:T(8,128)}, u32[]{:S(2)}) copy-start(f32[48,48,2,48]{3,1,2,0:T(8,128)} %bitcast_multiply_fusion.42) | copy-start | bytes 2654212 | tf_op jit(solution)/shard_map/while
  198.1 2.1 copy-start
  198.1 2.4 copy-start.1
  204.6 2.4 copy-start.29
  210.0 1.0 copy-start.30
  226.7 2.1 copy-start.12
  226.7 2.1 copy-start.15
  226.8 2.1 copy-start.16
  226.8 2.1 copy-start.28
  252.2 3.5 copy-start.6
  252.2 3.5 copy-start.7
  269.2 3.6 copy-start.17
  269.2 3.5 copy-start.18
  269.2 3.5 copy-start.24
  295.8 3.5 copy-start.10
  295.8 3.5 copy-start.11
  313.0 3.6 copy-start.13
  313.0 3.6 copy-start.14
  313.0 3.6 copy-start.22
  313.0 3.6 copy-start.26
  337.0 2.1 copy-start.8
  337.0 2.1 copy-start.9
  352.5 3.5 copy-start.4
  352.5 3.5 copy-start.5
  363.4 8.3 %copy-start.2 = (f32[48,48,2,48]{3,1,2,0:T(8,128)S(1)}, f32[48,48,2,48]{3,1,2,0:T(8,128)}, u32[]{:S(2)}) copy-start(f32[48,48,2,48]{3,1,2,0:T(8,128)} %bitcast_multiply_fusion.41) | copy-start | bytes 2654212 | tf_op jit(solution)/shard_map/while
  363.5 8.3 %copy-start.3 = (f32[48,48,2,48]{3,1,2,0:T(8,128)S(1)}, f32[48,48,2,48]{3,1,2,0:T(8,128)}, u32[]{:S(2)}) copy-start(f32[48,48,2,48]{3,1,2,0:T(8,128)} %bitcast_multiply_fusion.42) | copy-start | bytes 2654212 | tf_op jit(solution)/shard_map/while
  369.6 2.1 copy-start
  369.6 2.4 copy-start.1
  376.2 2.4 copy-start.29
  381.6 1.0 copy-start.30
  386.5 4.4 %copy-start.19 = (f32[16,6,2304]{2,0,1:T(8,128)S(1)}, f32[16,6,2304]{2,0,1:T(8,128)}, u32[]{:S(2)}) copy-start(f32[16,6,2304]{2,0,1:T(8,128)} %param.6) | copy-start | bytes 2654212
  386.5 7.1 %copy-start.34 = (s32[64]{0:T(128)S(1)}, s32[64]{0:T(128)}, u32[]{:S(2)}) copy-start(s32[64]{0:T(128)} %param.8) | copy-start | bytes 772
  386.5 26.5 %all-to-all-start.1 = ((f32[2,48,2304]{2,0,1:T(2,128)}), f32[2,48,2304]{2,0,1:T(2,128)}, u32[]{:S(2)}, u32[]{:S(2)}) async-start(f32[2,48,2304]{2,0,1:T(2,128)} %get-tuple-element.142), calls=%async_computation.1 | async-start | bytes 1769472 | tf_op jit(solution)/shard_map/all_to_all | solution.py:142
  391.0 26.1 %collective-permute-start = (f32[1,6,2304]{2,0,1:T(1,128)S(1)}, f32[1,6,2304]{2,0,1:T(1,128)S(1)}, u32[]{:S(2)}, u32[]{:S(2)}) collective-permute-start(f32[1,6,2304]{2,0,1:T(1,128)S(1)} %get-tuple-element.523), channel_id=1, source_target_pairs={{0,8},{8,16},{16,24},{1,9},{9,17},{17,25},{2,10},{10,18},{18,26},{... | collective-permute-start | bytes 165896 | tf_op jit(solution)/shard_map/ppermute | solution.py:34
  392.3 24.9 %collective-permute-start.1 = (f32[1,6,2304]{2,0,1:T(1,128)S(1)}, f32[1,6,2304]{2,0,1:T(1,128)S(1)}, u32[]{:S(2)}, u32[]{:S(2)}) collective-permute-start(f32[1,6,2304]{2,0,1:T(1,128)S(1)} %get-tuple-element.524), channel_id=1, source_target_pairs={{8,0},{16,8},{24,16},{9,1},{17,9},{25,17},{10,2},{18,10},{26,18},{... | collective-permute-start | bytes 165896 | tf_op jit(solution)/shard_map/ppermute | solution.py:36
  415.3 1.9 copy-start.20
  415.3 1.9 copy-start.33
where the time goes:
time: 423 us; the launch traced here: 419 us
  matrix products  196 us (46%)
  local copies, waits for them, and re-layouts  94.8 us (22%)
  other arithmetic  82.4 us (19%)
  waiting for transfers between devices  25.3 us (6%)
  starting transfers between devices  14.2 us (3%)
  loops' own time  5.29 us (1%)
    dot_general x48, matrix products, apply_table(): lax.dot_general(tensor, table, ((dims, tuple(range(len(dims)))), ((), ())...  196 us
    dot_general x16, local copies, waits for them, and re-layouts, apply_table(): lax.dot_general(tensor, table, ((dims, tuple(range(len(dims)))), ((), ())...  61 us
    sub x6, other arithmetic, packed(): joined_real = first_factor * real_part - second_factor * imag_part  58.4 us
    all_to_all x1, waiting for transfers between devices, body(): lax.all_to_all(distribution, 'vel', split_axis=0, concat_axis=1, tiled=True)  14.4 us
    div x1, other arithmetic, kernel_tables(): loss_total = sum(loss_tables) / 6.0  13.5 us
    all_to_all x1, waiting for transfers between devices, body(): lax.all_to_all(cell_terms, 'vel', split_axis=1, concat_axis=0, tiled=True)  10.9 us
  transfers between devices with their start and end apart: 4, of which 2 were waited for; matrix products, arithmetic and copies ran while one was open for 6% of the time, Pallas kernels for 0%

commit v1 on v0

v1 whole, which is shorter than its diff:
```python
import math

import jax
import jax.numpy as jnp
import ml_dtypes
import numpy as np
from jax import lax
from jax.experimental import pallas as pl
from jax.experimental.pallas import tpu as pltpu
from jax.sharding import PartitionSpec as P

NV = 48
LENGTH = 8.0
RADIUS = 6.0
COURANT = 0.9
GOLDEN = (1.0 + math.sqrt(5.0)) / 2.0
SCALE = math.sqrt(1.0 + GOLDEN * GOLDEN)
HALF = 64
LANES = 128
BF = jnp.bfloat16


def real_basis():
    j = np.arange(NV)
    q = np.zeros((NV, NV))
    for f in range(25):
        q[f] = np.cos(2 * np.pi * f * j / NV) * (1.0 if f in (0, 24) else math.sqrt(2.0))
    for f in range(1, 24):
        q[24 + f] = np.sin(2 * np.pi * f * j / NV) * math.sqrt(2.0)
    q /= math.sqrt(NV)
    odd = np.zeros((NV, NV))
    for f in range(1, 24):
        odd[:, f] = -q[24 + f]
        odd[:, 24 + f] = q[f]
    mag = np.concatenate([np.arange(24), [0], np.arange(1, 24)]) * (math.pi / LENGTH)
    return q, odd, mag


def circulants():
    j = np.arange(NV)
    k = np.where(j < 24, j, np.where(j == 24, 0, j - NV))
    xi = k * (math.pi / LENGTH)
    f = np.fft.fft(np.eye(NV), axis=0)

    def real(mult):
        return np.real(np.fft.ifft(mult[:, None] * f, axis=0))

    result = []
    for length in (1.0 / SCALE, GOLDEN / SCALE):
        angle = 0.5 * RADIUS * xi * length
        result.append((real(np.cos(angle)), real(1j * np.sin(angle))))
    return result


def split_np(w):
    w = np.asarray(w, np.float32)
    hi = w.astype(ml_dtypes.bfloat16)
    lo = (w - hi.astype(np.float32)).astype(ml_dtypes.bfloat16)
    return hi, lo


def left(w):
    hi, lo = split_np(w)
    return np.concatenate([hi, hi, lo], axis=1)


def right(w):
    full = np.zeros((LANES, LANES))
    full[:NV, :NV] = w.T
    full[HALF : HALF + NV, HALF : HALF + NV] = w.T
    hi, lo = split_np(full)
    return np.concatenate([hi, hi, lo], axis=0)


def build_tables():
    q, odd, mag = real_basis()
    (c1, d1), (c2, d2) = circulants()
    mz, mx, my = mag[:, None, None], mag[None, :, None], mag[None, None, :]
    square = mz * mz + mx * mx + my * my

    def sinc(p):
        return np.sinc(RADIUS * np.sqrt(np.maximum(square - p * p, 0.0)) / (2.0 * math.pi))

    plus, minus = [], []
    for first, second in ((my, mz), (mx, my), (mz, mx)):
        same = sinc((first + GOLDEN * second) / SCALE)
        other = sinc((GOLDEN * second - first) / SCALE)
        plus.append((same + other) / 6.0)
        minus.append((other - same) / 6.0)
    spec = np.zeros((6, NV, NV, LANES), np.float32)
    values = np.stack(plus + minus)
    spec[..., :NV] = values
    spec[..., HALF : HALF + NV] = values
    lefts = [q, q.T, odd, c1, d1, c2, d2]
    left_all = np.stack([left(w) for w in lefts])
    left_pair = left(np.concatenate([c2, d2], axis=0))
    right_first = np.concatenate([right(w) for w in (q, c2, d2)], axis=1)
    right_rest = np.stack([right(q.T), right(odd)])
    right_gain = np.concatenate([right(c1), right(d1)], axis=1)
    return spec, left_all, left_pair, right_first, right_rest, right_gain


def parts(x):
    hi = x.astype(BF)
    lo = (x - hi.astype(jnp.float32)).astype(BF)
    return hi, lo


def tall(x):
    hi, lo = parts(x)
    return jnp.concatenate([hi, lo, hi], axis=0)


def wide(x):
    hi, lo = parts(x)
    return jnp.concatenate([hi, lo, hi], axis=1)


def dot(a, b):
    return jnp.dot(a, b, preferred_element_type=jnp.float32)


def collide_kernel(
    u_in, spec_hbm, la, lp, rf, rr, rg, out, u, v, ey, fy, spec, fields, gains, sem
):
    cells = u_in.shape[0]
    load = pltpu.make_async_copy(spec_hbm, spec, sem)
    load.start()
    u[...] = jnp.zeros_like(u)
    for x in range(NV):
        for c in range(cells):
            u[x * NV : (x + 1) * NV, c * HALF : c * HALF + NV] = u_in[c, :, x * NV : (x + 1) * NV]

    def first(x, carry):
        rows = pl.ds(pl.multiple_of(x * NV, NV), NV)
        three = dot(wide(u[rows, :]), rf[...])
        ey[rows, :] = three[:, LANES : 2 * LANES]
        fy[rows, :] = three[:, 2 * LANES :]
        v[rows, :] = dot(la[0], tall(three[:, :LANES]))
        return carry

    lax.fori_loop(0, NV, first, 0, unroll=2)
    load.wait()

    def second(z, carry):
        rows = pl.ds(z, NV, stride=NV)
        s = dot(la[0], tall(v[rows, :]))
        hat = [tall(s * spec[f, z]) for f in range(6)]
        even = dot(la[1], jnp.concatenate(hat[:4], axis=1))
        odd = dot(la[2], jnp.concatenate(hat[4:], axis=1))
        for f in range(4):
            fields[f, rows, :] = even[:, f * LANES : (f + 1) * LANES]
        for f in range(2):
            fields[4 + f, rows, :] = odd[:, f * LANES : (f + 1) * LANES]
        pair = dot(lp[...], tall(u[rows, :]))
        gains[0, rows, :] = dot(la[3], tall(ey[rows, :]))
        gains[1, rows, :] = dot(la[4], tall(fy[rows, :]))
        gains[2, rows, :] = pair[:NV]
        gains[3, rows, :] = pair[NV:]
        return carry

    lax.fori_loop(0, NV, second, 0, unroll=2)

    def third(x, carry):
        rows = pl.ds(pl.multiple_of(x * NV, NV), NV)
        even_in = [wide(fields[f, rows, :]) for f in (0, 1, 2, 5)]
        odd_in = [wide(fields[f, rows, :]) for f in (3, 4)]
        even = dot(jnp.concatenate(even_in, axis=0), rr[0])
        odd = dot(jnp.concatenate(odd_in, axis=0), rr[1])
        plus = [even[f * NV : (f + 1) * NV] for f in range(3)]
        minus_zx = even[3 * NV :]
        minus_yz, minus_xy = odd[:NV], odd[NV:]
        straight = dot(
            la[1], jnp.concatenate([tall(p) for p in plus] + [tall(minus_xy)], axis=1)
        )
        turned = dot(la[2], jnp.concatenate([tall(minus_yz), tall(minus_zx)], axis=1))
        cell = u[rows, :]
        along = dot(wide(cell), rg[...])
        gain_yz = dot(la[5], tall(along[:, :LANES]))
        swap_yz = dot(la[6], tall(along[:, LANES:]))
        gain_zx = dot(la[3], tall(gains[2, rows, :]))
        swap_zx = dot(la[4], tall(gains[3, rows, :]))
        total = (gain_yz - cell) * straight[:, :LANES]
        total += swap_yz * turned[:, :LANES]
        total += (gains[0, rows, :] - cell) * straight[:, LANES : 2 * LANES]
        total += gains[1, rows, :] * straight[:, 3 * LANES :]
        total += (gain_zx - cell) * straight[:, 2 * LANES : 3 * LANES]
        total += swap_zx * turned[:, LANES:]
        v[rows, :] = total
        return carry

    lax.fori_loop(0, NV, third, 0, unroll=2)
    for x in range(NV):
        for c in range(cells):
            out[c, :, x * NV : (x + 1) * NV] = v[x * NV : (x + 1) * NV, c * HALF : c * HALF + NV]


def collide(cells):
    tables = build_tables()
    vmem = pl.BlockSpec(memory_space=pltpu.VMEM)
    size = (NV * NV, LANES)
    return pl.pallas_call(
        collide_kernel,
        out_shape=jax.ShapeDtypeStruct(cells.shape, jnp.float32),
        in_specs=[vmem, pl.BlockSpec(memory_space=pl.ANY)] + [vmem] * 5,
        out_specs=vmem,
        scratch_shapes=[
            pltpu.VMEM(size, jnp.float32),
            pltpu.VMEM(size, jnp.float32),
            pltpu.VMEM(size, jnp.float32),
            pltpu.VMEM(size, jnp.float32),
            pltpu.VMEM((6, NV, NV, LANES), jnp.float32),
            pltpu.VMEM((6,) + size, jnp.float32),
            pltpu.VMEM((4,) + size, jnp.float32),
            pltpu.SemaphoreType.DMA,
        ],
        compiler_params=pltpu.CompilerParams(vmem_limit_bytes=48 * 1024 * 1024),
        cost_estimate=pl.CostEstimate(
            flops=10**9, bytes_accessed=10 * 2**20, transcendentals=0
        ),
    )(cells, *[jnp.asarray(t) for t in tables])


def padded_2(cells, sides, width):
    for axis, dim in sides:
        count = lax.axis_size(axis)
        ends = count - 1
        head = lax.slice_in_dim(cells, 0, width, axis=dim)
        tail = lax.slice_in_dim(cells, cells.shape[dim] - width, cells.shape[dim], axis=dim)
        cells = jnp.concatenate(
            [
                lax.ppermute(tail, axis, [(i, (i + 1) % count) for i in range(ends)]),
                cells,
                lax.ppermute(head, axis, [((i + 1) % count, i) for i in range(ends)]),
            ],
            axis=dim,
        )
    return cells


def body(distribution, collision_rate, face_flags):
    cell_count, planes_dev, width = distribution.shape
    points = NV
    regrouped = lax.all_to_all(distribution, "vel", split_axis=0, concat_axis=1, tiled=True)
    own = regrouped.shape[0]
    terms = [collide(regrouped[i : min(i + 2, own)]) for i in range(0, own, 2)]
    cell_terms = terms[0] if len(terms) == 1 else jnp.concatenate(terms, axis=0)
    collision_term = lax.all_to_all(cell_terms, "vel", split_axis=1, concat_axis=0, tiled=True)
    offset = lax.axis_index("space") * cell_count
    padded = padded_2(distribution, (("space", 0),), 1)
    mirror = distribution.reshape(cell_count, planes_dev, points, points)[:, :, ::-1, :].reshape(
        cell_count, planes_dev, width
    )
    wall_flags = jnp.concatenate([face_flags, jnp.ones((1,), jnp.int32)])
    nearby_walls = lax.dynamic_slice_in_dim(wall_flags, offset, cell_count + 1)
    lower_wall = (nearby_walls[:-1] == 1)[:, None, None]
    upper_wall = (nearby_walls[1:] == 1)[:, None, None]
    at_start = (offset + jnp.arange(cell_count, dtype=jnp.int32) == 0)[:, None, None]
    lower_side = jnp.where(lower_wall, mirror, jnp.where(at_start, distribution, padded[:-2]))
    upper_side = jnp.where(upper_wall, mirror, padded[2:])
    column = (jnp.arange(width, dtype=jnp.int32) // points).astype(jnp.float32)
    centre = (points - 1) / 2.0
    speed = COURANT * (column - centre) / centre
    upwind_flux = jnp.where(
        speed > 0, speed * (distribution - lower_side), speed * (upper_side - distribution)
    )
    return distribution - upwind_flux + collision_rate[:, None, None] * collision_term


def solution(mesh):
    return jax.shard_map(
        body,
        mesh=mesh,
        in_specs=(P("space", "vel", None), P("space"), P()),
        out_specs=P("space", "vel", None),
        check_vma=False,
    )
```

time: 423 us -> 121 us (0.29)
  matrix products: 196 us -> 0 us
  other arithmetic: 82.4 us -> 3.08 us
  local copies, waits for them, and re-layouts: 94.8 us -> 15.5 us
  Pallas kernels: 0 us -> 50 us
  blocking collectives: 0 us -> 36 us
  waiting for transfers between devices: 25.3 us -> 6.59 us
  loops' own time: 5.29 us -> 0 us
  starting transfers between devices: 14.2 us -> 9.15 us
    dot_general x48 -> x0, matrix products: 196 us -> none  [apply_table(): lax.dot_general(tensor, table, ((dims, tuple(range(len(dims)))), ((), ())...]
    sub x8 -> x0, other arithmetic: 66.7 us -> none  [the longest x6 58.4 us: packed(): joined_real = first_factor * real_part - second_factor * imag_part]
    dot_general x16 -> x0, local copies, waits for them, and re-layouts: 61 us -> none  [apply_table(): lax.dot_general(tensor, table, ((dims, tuple(range(len(dims)))), ((), ())...]
    pallas_call x0 -> x1, Pallas kernels: none -> 50 us  [collide(): pl.pallas_call(collide_kernel, out_shape=jax.ShapeDtypeStruct(cells.shape...]
    all_to_all x0 -> x1, blocking collectives: none -> 36 us  [body(): lax.all_to_all(distribution, 'vel', split_axis=0, concat_axis=1, tiled=True)]
    all_to_all x1 -> x0, waiting for transfers between devices: 14.4 us -> none  [body(): lax.all_to_all(distribution, 'vel', split_axis=0, concat_axis=1, tiled=True)]
    div x1 -> x0, other arithmetic: 13.5 us -> none  [kernel_tables(): loss_total = sum(loss_tables) / 6.0]
    all_to_all x1 -> x0, starting transfers between devices: 7.25 us -> none  [body(): lax.all_to_all(distribution, 'vel', split_axis=0, concat_axis=1, tiled=True)]
  transfers between devices with their start and end apart: 4 -> 3, of which waited for: 2 -> 1; matrix products, arithmetic and copies ran while one was open for 6% -> 9% of each run, Pallas kernels for 0% -> 0%
where the time goes in v1:
time: 121 us; the launch traced here: 120 us
  Pallas kernels  50 us (41%)
  blocking collectives  36 us (30%)
  local copies, waits for them, and re-layouts  15.5 us (13%)
  starting transfers between devices  9.15 us (8%)
  waiting for transfers between devices  6.59 us (5%)
  other arithmetic  3.08 us (3%)
    pallas_call x1, Pallas kernels, collide(): pl.pallas_call(collide_kernel, out_shape=jax.ShapeDtypeStruct(cells.shape...  50 us
    all_to_all x1, blocking collectives, body(): lax.all_to_all(distribution, 'vel', split_axis=0, concat_axis=1, tiled=True)  36 us
    all_to_all x1, waiting for transfers between devices, body(): lax.all_to_all(cell_terms, 'vel', split_axis=1, concat_axis=0, tiled=True)  6.59 us
    reshape x2, local copies, waits for them, and re-layouts, body(): distribution.reshape(cell_count, planes_dev, points, points)[:, :, ::-1, :]  4.81 us
    all_to_all x1, starting transfers between devices, body(): lax.all_to_all(cell_terms, 'vel', split_axis=1, concat_axis=0, tiled=True)  4.22 us
    ppermute x1, starting transfers between devices, padded_2(): lax.ppermute(tail, axis, [(i, (i + 1) % count) for i in range(ends)])  3.65 us
    rev x1, local copies, waits for them, and re-layouts, body(): distribution.reshape(cell_count, planes_dev, points, points)[:, :, ::-1, :]  3.49 us
  transfers between devices with their start and end apart: 3, of which 1 were waited for; matrix products, arithmetic and copies ran while one was open for 9% of the time, Pallas kernels for 0%

profile of v1, /device:TPU:0, one launch (start us, length us, event | category | flops | bytes accessed | tf_op | source)
XLA Modules:
  0.0 120.4 jit_solution(14569949696039530543)
XLA Ops:
  0.0 1.7 %copy.19 = f32[16,6,2304]{2,1,0:T(8,128)S(1)} copy(f32[16,6,2304]{2,0,1:T(8,128)} %param.9) | data formatting | bytes 1769472 | tf_op args[0]
  1.7 36.0 %all_to_all.36 = f32[16,6,2304]{2,1,0:T(8,128)S(1)} all-to-all(f32[16,6,2304]{2,1,0:T(8,128)S(1)} %copy.19), channel_id=1, replica_groups=mesh['space'=4,'vel'=8] {'vel'}, dimensions={0} | all-to-all | bytes 1769472 | tf_op jit(solution)/shard_map/all_to_all | solution.py:244
  37.7 0.0 copy-start
  37.7 0.0 copy-start.1
  37.7 0.0 copy-start.2
  37.7 0.0 copy-start.3
  37.7 0.0 copy-start.4
  37.7 0.5 copy.20
  38.2 0.1 copy.21.u_in
  38.3 0.4 copy-done
  38.7 0.1 copy-done.1
  38.7 0.1 copy-done.2
  38.8 0.1 copy-done.3
  38.9 0.0 copy-done.4
  38.9 50.0 %shard_map.91 = f32[2,48,2304]{2,1,0:T(8,128)S(1)} custom-call(f32[2,48,2304]{2,1,0:T(8,128)S(1)} %copy.21.u_in, f32[6,48,48,128]{3,2,1,0:T(8,128)} %constant.46.clone.spec_hbm, bf16[7,48,144]{2,1,0:T(8,128)(2,1)S(1)} %copy-done.3, bf16[96,144]{1,0:T(8,128)(2,1)S(1)} %copy-done.4, bf16[384,384]{1,0:T(8,128)(2,1)S(1)} %copy-done, ...), custom_call_target="tpu_custom_call" | custom-call | flops 1000000000 | bytes 10485760 | tf_op jit(solution)/shard_map/pallas_call | solution.py:202
  88.9 0.0 copy-start.5
  88.9 0.0 copy-start.7
  88.9 1.6 %copy.22 = f32[2,48,2304]{2,0,1:T(2,128)} copy(f32[2,48,2304]{2,1,0:T(8,128)S(1)} %shard_map.91) | data formatting | bytes 1769472 | tf_op jit(solution)/shard_map/pallas_call | solution.py:202
  90.6 4.2 %all-to-all-start.1 = ((f32[2,48,2304]{2,0,1:T(2,128)}), f32[2,48,2304]{2,0,1:T(2,128)}, u32[]{:S(2)}, u32[]{:S(2)}) async-start(f32[2,48,2304]{2,0,1:T(2,128)} %copy.22), calls=%async_computation.1 | async-start | bytes 1769472 | tf_op jit(solution)/shard_map/all_to_all | solution.py:248
  94.8 0.0 copy-done.5
  94.8 0.7 fusion.16
  95.5 1.3 %collective-permute-start.1 = (f32[1,6,2304]{2,0,1:T(1,128)}, f32[1,6,2304]{2,0,1:T(1,128)}, u32[]{:S(2)}, u32[]{:S(2)}) collective-permute-start(f32[1,6,2304]{2,0,1:T(1,128)} %get-tuple-element.6), channel_id=1, source_target_pairs={{8,0},{16,8},{24,16},{9,1},{17,9},{25,17},{10,2},{18,10},{26,18},{... | collective-permute-start | bytes 165896 | tf_op jit(solution)/shard_map/ppermute | solution.py:234
  96.8 3.7 %collective-permute-start = (f32[1,6,2304]{2,0,1:T(1,128)}, f32[1,6,2304]{2,0,1:T(1,128)}, u32[]{:S(2)}, u32[]{:S(2)}) collective-permute-start(f32[1,6,2304]{2,0,1:T(1,128)} %get-tuple-element.5), channel_id=1, source_target_pairs={{0,8},{8,16},{16,24},{1,9},{9,17},{17,25},{2,10},{10,18},{18,26},{... | collective-permute-start | bytes 165896 | tf_op jit(solution)/shard_map/ppermute | solution.py:232
  100.4 0.0 copy-done.7
  100.4 0.1 pad_add_fusion
  100.5 0.1 dynamic_slice.3
  100.6 0.7 slice_compare_fusion.1
  101.3 2.9 %reshape.30 = f32[16,6,48,48]{3,2,0,1:T(8,128)} reshape(f32[16,6,2304]{2,0,1:T(8,128)S(1)} %copy-done.5) | data formatting | bytes 1769472 | tf_op jit(solution)/shard_map/reshape | solution.py:251
  104.2 3.5 %rev.3 = f32[16,6,48,48]{3,2,0,1:T(8,128)S(1)} reverse(f32[16,6,48,48]{3,2,0,1:T(8,128)} %reshape.30), dimensions={2} | reverse | bytes 1769472 | tf_op jit(solution)/shard_map/rev | solution.py:251
  107.7 1.9 %reshape.31 = f32[16,6,2304]{2,0,1:T(8,128)} reshape(f32[16,6,48,48]{3,2,0,1:T(8,128)S(1)} %rev.3) | data formatting | bytes 1769472 | tf_op jit(solution)/shard_map/reshape | solution.py:251
  109.6 0.0 copy-start.6
  109.6 6.6 %all-to-all-done.1 = f32[2,48,2304]{2,0,1:T(2,128)} async-done(((f32[2,48,2304]{2,0,1:T(2,128)}), f32[2,48,2304]{2,0,1:T(2,128)}, u32[]{:S(2)}, u32[]{:S(2)}) %all-to-all-start.1) | async-done | bytes 884768 | tf_op jit(solution)/shard_map/all_to_all | solution.py:248
  116.2 1.3 %copy.23 = f32[8,2,6,2304]{3,1,0,2:T(2,128)S(1)} copy(f32[8,2,6,2304]{3,1,2,0:T(2,128)} %bitcast.4) | data formatting | bytes 1769472 | tf_op jit(solution)/shard_map/all_to_all | solution.py:248
  117.4 0.6 all_to_all.33
  118.1 0.0 collective-permute-done.1
  118.1 0.0 collective-permute-done
  118.1 0.0 copy-done.6
  118.1 2.3 %fusion.5 = f32[16,6,2304]{2,0,1:T(8,128)} fusion(f32[16,6,2304]{2,0,1:T(8,128)S(1)} %copy-done.5, f32[16,6,2304]{2,0,1:T(8,128)S(1)} %copy-done.6, f32[1,6,2304]{2,0,1:T(1,128)} %collective-permute-done.1, f32[1,6,2304]{2,0,1:T(1,128)} %collective-permute-done, f32[16,6,2304]{2,0,1:T(8,128)S(1)} %all_to_all.33, f32[16]{0:T(128)} %param.10, ...), kind=kLoop, calls=%fused_computation.6 | loop fusion | flops 2875392 | bytes 3661168 | tf_op jit(solution)/shard_map/add | solution.py:267
  (2 shorter events, 0.0 us)
Async XLA Ops:
  37.7 1.0 copy-start
  37.7 1.0 copy-start.1
  37.7 1.1 copy-start.2
  37.7 1.2 copy-start.3
  37.7 1.2 copy-start.4
  88.9 5.9 %copy-start.5 = (f32[16,6,2304]{2,0,1:T(8,128)S(1)}, f32[16,6,2304]{2,0,1:T(8,128)}, u32[]{:S(2)}) copy-start(f32[16,6,2304]{2,0,1:T(8,128)} %param.9) | copy-start | bytes 2654212
  88.9 11.5 %copy-start.7 = (s32[64]{0:T(128)S(1)}, s32[64]{0:T(128)}, u32[]{:S(2)}) copy-start(s32[64]{0:T(128)} %param.11) | copy-start | bytes 772
  90.6 25.6 %all-to-all-start.1 = ((f32[2,48,2304]{2,0,1:T(2,128)}), f32[2,48,2304]{2,0,1:T(2,128)}, u32[]{:S(2)}, u32[]{:S(2)}) async-start(f32[2,48,2304]{2,0,1:T(2,128)} %copy.22), calls=%async_computation.1 | async-start | bytes 1769472 | tf_op jit(solution)/shard_map/all_to_all | solution.py:248
  95.5 22.6 %collective-permute-start.1 = (f32[1,6,2304]{2,0,1:T(1,128)}, f32[1,6,2304]{2,0,1:T(1,128)}, u32[]{:S(2)}, u32[]{:S(2)}) collective-permute-start(f32[1,6,2304]{2,0,1:T(1,128)} %get-tuple-element.6), channel_id=1, source_target_pairs={{8,0},{16,8},{24,16},{9,1},{17,9},{25,17},{10,2},{18,10},{26,18},{... | collective-permute-start | bytes 165896 | tf_op jit(solution)/shard_map/ppermute | solution.py:234
  96.8 21.3 %collective-permute-start = (f32[1,6,2304]{2,0,1:T(1,128)}, f32[1,6,2304]{2,0,1:T(1,128)}, u32[]{:S(2)}, u32[]{:S(2)}) collective-permute-start(f32[1,6,2304]{2,0,1:T(1,128)} %get-tuple-element.5), channel_id=1, source_target_pairs={{0,8},{8,16},{16,24},{1,9},{9,17},{17,25},{2,10},{10,18},{18,26},{... | collective-permute-start | bytes 165896 | tf_op jit(solution)/shard_map/ppermute | solution.py:232
  109.6 8.5 %copy-start.6 = (f32[16,6,2304]{2,0,1:T(8,128)S(1)}, f32[16,6,2304]{2,0,1:T(8,128)}, u32[]{:S(2)}) copy-start(f32[16,6,2304]{2,0,1:T(8,128)} %reshape.31) | copy-start | bytes 2654212

commit v2 on v1

--- a/solution.py
+++ b/solution.py
@@ -17,6 +17,7 @@
 SCALE = math.sqrt(1.0 + GOLDEN * GOLDEN)
 HALF = 64
 LANES = 128
+BATCH = 4
 BF = jnp.bfloat16
 
 
@@ -120,6 +121,12 @@
     return jnp.dot(a, b, preferred_element_type=jnp.float32)
 
 
+def each(w, x):
+    blocks = [tall(x[i * NV : (i + 1) * NV]) for i in range(BATCH)]
+    result = dot(w, jnp.concatenate(blocks, axis=1))
+    return jnp.concatenate([result[:, i * LANES : (i + 1) * LANES] for i in range(BATCH)], axis=0)
+
+
 def collide_kernel(
     u_in, spec_hbm, la, lp, rf, rr, rg, out, u, v, ey, fy, spec, fields, gains, sem
 ):
@@ -131,15 +138,16 @@
         for c in range(cells):
             u[x * NV : (x + 1) * NV, c * HALF : c * HALF + NV] = u_in[c, :, x * NV : (x + 1) * NV]
 
-    def first(x, carry):
-        rows = pl.ds(pl.multiple_of(x * NV, NV), NV)
+    def first(group, carry):
+        start = pl.multiple_of(group * BATCH * NV, BATCH * NV)
+        rows = pl.ds(start, BATCH * NV)
         three = dot(wide(u[rows, :]), rf[...])
         ey[rows, :] = three[:, LANES : 2 * LANES]
         fy[rows, :] = three[:, 2 * LANES :]
-        v[rows, :] = dot(la[0], tall(three[:, :LANES]))
+        v[rows, :] = each(la[0], three[:, :LANES])
         return carry
 
-    lax.fori_loop(0, NV, first, 0, unroll=2)
+    lax.fori_loop(0, NV // BATCH, first, 0)
     load.wait()
 
     def second(z, carry):
@@ -159,37 +167,28 @@
         gains[3, rows, :] = pair[NV:]
         return carry
 
-    lax.fori_loop(0, NV, second, 0, unroll=2)
-
-    def third(x, carry):
-        rows = pl.ds(pl.multiple_of(x * NV, NV), NV)
+    lax.fori_loop(0, NV, second, 0, unroll=4)
+
+    def third(group, carry):
+        count = BATCH * NV
+        start = pl.multiple_of(group * count, count)
+        rows = pl.ds(start, count)
         even_in = [wide(fields[f, rows, :]) for f in (0, 1, 2, 5)]
         odd_in = [wide(fields[f, rows, :]) for f in (3, 4)]
         even = dot(jnp.concatenate(even_in, axis=0), rr[0])
         odd = dot(jnp.concatenate(odd_in, axis=0), rr[1])
-        plus = [even[f * NV : (f + 1) * NV] for f in range(3)]
-        minus_zx = even[3 * NV :]
-        minus_yz, minus_xy = odd[:NV], odd[NV:]
-        straight = dot(
-            la[1], jnp.concatenate([tall(p) for p in plus] + [tall(minus_xy)], axis=1)
-        )
-        turned = dot(la[2], jnp.concatenate([tall(minus_yz), tall(minus_zx)], axis=1))
         cell = u[rows, :]
         along = dot(wide(cell), rg[...])
-        gain_yz = dot(la[5], tall(along[:, :LANES]))
-        swap_yz = dot(la[6], tall(along[:, LANES:]))
-        gain_zx = dot(la[3], tall(gains[2, rows, :]))
-        swap_zx = dot(la[4], tall(gains[3, rows, :]))
-        total = (gain_yz - cell) * straight[:, :LANES]
-        total += swap_yz * turned[:, :LANES]
-        total += (gains[0, rows, :] - cell) * straight[:, LANES : 2 * LANES]
-        total += gains[1, rows, :] * straight[:, 3 * LANES :]
-        total += (gain_zx - cell) * straight[:, 2 * LANES : 3 * LANES]
-        total += swap_zx * turned[:, LANES:]
+        total = (each(la[5], along[:, :LANES]) - cell) * each(la[1], even[:count])
+        total += each(la[6], along[:, LANES:]) * each(la[2], odd[:count])
+        total += (gains[0, rows, :] - cell) * each(la[1], even[count : 2 * count])
+        total += gains[1, rows, :] * each(la[1], odd[count:])
+        total += (each(la[3], gains[2, rows, :]) - cell) * each(la[1], even[2 * count : 3 * count])
+        total += each(la[4], gains[3, rows, :]) * each(la[2], even[3 * count :])
         v[rows, :] = total
         return carry
 
-    lax.fori_loop(0, NV, third, 0, unroll=2)
+    lax.fori_loop(0, NV // BATCH, third, 0)
     for x in range(NV):
         for c in range(cells):
             out[c, :, x * NV : (x + 1) * NV] = v[x * NV : (x + 1) * NV, c * HALF : c * HALF + NV]

time: 121 us -> 100 us (0.83)
  Pallas kernels: 50 us -> 29.4 us
    pallas_call x1, Pallas kernels: 50 us -> 29.4 us  [collide(): pl.pallas_call(collide_kernel, out_shape=jax.ShapeDtypeStruct(cells.shape...]
  transfers between devices with their start and end apart: 3 -> 3, of which waited for: 1 -> 1; matrix products, arithmetic and copies ran while one was open for 9% -> 11% of each run, Pallas kernels for 0% -> 0%
where the time goes in v2:
time: 100 us; the launch traced here: 99.8 us
  blocking collectives  36 us (36%)
  Pallas kernels  29.4 us (29%)
  local copies, waits for them, and re-layouts  15.5 us (16%)
  starting transfers between devices  9.15 us (9%)
  waiting for transfers between devices  6.59 us (7%)
  other arithmetic  3.08 us (3%)
    all_to_all x1, blocking collectives, body(): lax.all_to_all(distribution, 'vel', split_axis=0, concat_axis=1, tiled=True)  36 us
    pallas_call x1, Pallas kernels, collide(): pl.pallas_call(collide_kernel, out_shape=jax.ShapeDtypeStruct(cells.shape...  29.4 us
    all_to_all x1, waiting for transfers between devices, body(): lax.all_to_all(cell_terms, 'vel', split_axis=1, concat_axis=0, tiled=True)  6.59 us
    reshape x2, local copies, waits for them, and re-layouts, body(): distribution.reshape(cell_count, planes_dev, points, points)[:, :, ::-1, :]  4.81 us
    all_to_all x1, starting transfers between devices, body(): lax.all_to_all(cell_terms, 'vel', split_axis=1, concat_axis=0, tiled=True)  4.22 us
    ppermute x1, starting transfers between devices, padded_2(): lax.ppermute(tail, axis, [(i, (i + 1) % count) for i in range(ends)])  3.65 us
    rev x1, local copies, waits for them, and re-layouts, body(): distribution.reshape(cell_count, planes_dev, points, points)[:, :, ::-1, :]  3.49 us
    unnamed x17, local copies, waits for them, and re-layouts  2.37 us
  transfers between devices with their start and end apart: 3, of which 1 were waited for; matrix products, arithmetic and copies ran while one was open for 11% of the time, Pallas kernels for 0%

profile of v2, /device:TPU:0, one launch (start us, length us, event | category | flops | bytes accessed | tf_op | source)
XLA Modules:
  0.0 99.8 jit_solution(17988461900676412910)
XLA Ops:
  0.0 1.7 %copy.19 = f32[16,6,2304]{2,1,0:T(8,128)S(1)} copy(f32[16,6,2304]{2,0,1:T(8,128)} %param.9) | data formatting | bytes 1769472 | tf_op args[0]
  1.7 36.0 %all_to_all.36 = f32[16,6,2304]{2,1,0:T(8,128)S(1)} all-to-all(f32[16,6,2304]{2,1,0:T(8,128)S(1)} %copy.19), channel_id=1, replica_groups=mesh['space'=4,'vel'=8] {'vel'}, dimensions={0} | all-to-all | bytes 1769472 | tf_op jit(solution)/shard_map/all_to_all | solution.py:243
  37.7 0.0 copy-start
  37.7 0.0 copy-start.1
  37.7 0.0 copy-start.2
  37.7 0.0 copy-start.3
  37.7 0.0 copy-start.4
  37.7 0.5 copy.20
  38.2 0.1 copy.21.u_in
  38.3 0.4 copy-done
  38.7 0.1 copy-done.1
  38.7 0.1 copy-done.2
  38.8 0.1 copy-done.3
  38.9 0.0 copy-done.4
  38.9 29.4 %shard_map.91 = f32[2,48,2304]{2,1,0:T(8,128)S(1)} custom-call(f32[2,48,2304]{2,1,0:T(8,128)S(1)} %copy.21.u_in, f32[6,48,48,128]{3,2,1,0:T(8,128)} %constant.46.clone.spec_hbm, bf16[7,48,144]{2,1,0:T(8,128)(2,1)S(1)} %copy-done.3, bf16[96,144]{1,0:T(8,128)(2,1)S(1)} %copy-done.4, bf16[384,384]{1,0:T(8,128)(2,1)S(1)} %copy-done, ...), custom_call_target="tpu_custom_call" | custom-call | flops 1000000000 | bytes 10485760 | tf_op jit(solution)/shard_map/pallas_call | solution.py:201
  68.3 0.0 copy-start.5
  68.3 0.0 copy-start.7
  68.3 1.6 %copy.22 = f32[2,48,2304]{2,0,1:T(2,128)} copy(f32[2,48,2304]{2,1,0:T(8,128)S(1)} %shard_map.91) | data formatting | bytes 1769472 | tf_op jit(solution)/shard_map/pallas_call | solution.py:201
  69.9 4.2 %all-to-all-start.1 = ((f32[2,48,2304]{2,0,1:T(2,128)}), f32[2,48,2304]{2,0,1:T(2,128)}, u32[]{:S(2)}, u32[]{:S(2)}) async-start(f32[2,48,2304]{2,0,1:T(2,128)} %copy.22), calls=%async_computation.1 | async-start | bytes 1769472 | tf_op jit(solution)/shard_map/all_to_all | solution.py:247
  74.2 0.0 copy-done.5
  74.2 0.7 fusion.16
  74.9 1.3 %collective-permute-start.1 = (f32[1,6,2304]{2,0,1:T(1,128)}, f32[1,6,2304]{2,0,1:T(1,128)}, u32[]{:S(2)}, u32[]{:S(2)}) collective-permute-start(f32[1,6,2304]{2,0,1:T(1,128)} %get-tuple-element.6), channel_id=1, source_target_pairs={{8,0},{16,8},{24,16},{9,1},{17,9},{25,17},{10,2},{18,10},{26,18},{... | collective-permute-start | bytes 165896 | tf_op jit(solution)/shard_map/ppermute | solution.py:233
  76.2 3.7 %collective-permute-start = (f32[1,6,2304]{2,0,1:T(1,128)}, f32[1,6,2304]{2,0,1:T(1,128)}, u32[]{:S(2)}, u32[]{:S(2)}) collective-permute-start(f32[1,6,2304]{2,0,1:T(1,128)} %get-tuple-element.5), channel_id=1, source_target_pairs={{0,8},{8,16},{16,24},{1,9},{9,17},{17,25},{2,10},{10,18},{18,26},{... | collective-permute-start | bytes 165896 | tf_op jit(solution)/shard_map/ppermute | solution.py:231
  79.8 0.0 copy-done.7
  79.8 0.1 pad_add_fusion
  79.9 0.1 dynamic_slice.3
  80.0 0.7 slice_compare_fusion.1
  80.7 2.9 %reshape.30 = f32[16,6,48,48]{3,2,0,1:T(8,128)} reshape(f32[16,6,2304]{2,0,1:T(8,128)S(1)} %copy-done.5) | data formatting | bytes 1769472 | tf_op jit(solution)/shard_map/reshape | solution.py:250
  83.6 3.5 %rev.3 = f32[16,6,48,48]{3,2,0,1:T(8,128)S(1)} reverse(f32[16,6,48,48]{3,2,0,1:T(8,128)} %reshape.30), dimensions={2} | reverse | bytes 1769472 | tf_op jit(solution)/shard_map/rev | solution.py:250
  87.1 1.9 %reshape.31 = f32[16,6,2304]{2,0,1:T(8,128)} reshape(f32[16,6,48,48]{3,2,0,1:T(8,128)S(1)} %rev.3) | data formatting | bytes 1769472 | tf_op jit(solution)/shard_map/reshape | solution.py:250
  89.0 0.0 copy-start.6
  89.0 6.6 %all-to-all-done.1 = f32[2,48,2304]{2,0,1:T(2,128)} async-done(((f32[2,48,2304]{2,0,1:T(2,128)}), f32[2,48,2304]{2,0,1:T(2,128)}, u32[]{:S(2)}, u32[]{:S(2)}) %all-to-all-start.1) | async-done | bytes 884768 | tf_op jit(solution)/shard_map/all_to_all | solution.py:247
  95.6 1.3 %copy.23 = f32[8,2,6,2304]{3,1,0,2:T(2,128)S(1)} copy(f32[8,2,6,2304]{3,1,2,0:T(2,128)} %bitcast.4) | data formatting | bytes 1769472 | tf_op jit(solution)/shard_map/all_to_all | solution.py:247
  96.8 0.6 all_to_all.33
  97.5 0.0 collective-permute-done.1
  97.5 0.0 collective-permute-done
  97.5 0.0 copy-done.6
  97.5 2.3 %fusion.5 = f32[16,6,2304]{2,0,1:T(8,128)} fusion(f32[16,6,2304]{2,0,1:T(8,128)S(1)} %copy-done.5, f32[16,6,2304]{2,0,1:T(8,128)S(1)} %copy-done.6, f32[1,6,2304]{2,0,1:T(1,128)} %collective-permute-done.1, f32[1,6,2304]{2,0,1:T(1,128)} %collective-permute-done, f32[16,6,2304]{2,0,1:T(8,128)S(1)} %all_to_all.33, f32[16]{0:T(128)} %param.10, ...), kind=kLoop, calls=%fused_computation.6 | loop fusion | flops 2875392 | bytes 3661168 | tf_op jit(solution)/shard_map/add | solution.py:266
  (2 shorter events, 0.0 us)
Async XLA Ops:
  37.7 1.0 copy-start
  37.7 1.0 %copy-start.1 = (bf16[2,384,128]{2,1,0:T(8,128)(2,1)S(1)}, bf16[2,384,128]{2,1,0:T(8,128)(2,1)}, u32[]{:S(2)}) copy-start(bf16[2,384,128]{2,1,0:T(8,128)(2,1)} %constant.50.clone.rr) | copy-start | bytes 589828
  37.7 1.1 %copy-start.2 = (bf16[384,256]{1,0:T(8,128)(2,1)S(1)}, bf16[384,256]{1,0:T(8,128)(2,1)}, u32[]{:S(2)}) copy-start(bf16[384,256]{1,0:T(8,128)(2,1)} %constant.51.clone.rg) | copy-start | bytes 589828
  37.7 1.2 %copy-start.3 = (bf16[7,48,144]{2,1,0:T(8,128)(2,1)S(1)}, bf16[7,48,144]{2,1,0:T(8,128)(2,1)}, u32[]{:S(2)}) copy-start(bf16[7,48,144]{2,1,0:T(8,128)(2,1)} %constant.47.clone.la) | copy-start | bytes 290308
  37.7 1.2 %copy-start.4 = (bf16[96,144]{1,0:T(8,128)(2,1)S(1)}, bf16[96,144]{1,0:T(8,128)(2,1)}, u32[]{:S(2)}) copy-start(bf16[96,144]{1,0:T(8,128)(2,1)} %constant.48.clone.lp) | copy-start | bytes 82948
  68.3 5.9 %copy-start.5 = (f32[16,6,2304]{2,0,1:T(8,128)S(1)}, f32[16,6,2304]{2,0,1:T(8,128)}, u32[]{:S(2)}) copy-start(f32[16,6,2304]{2,0,1:T(8,128)} %param.9) | copy-start | bytes 2654212
  68.3 11.5 %copy-start.7 = (s32[64]{0:T(128)S(1)}, s32[64]{0:T(128)}, u32[]{:S(2)}) copy-start(s32[64]{0:T(128)} %param.11) | copy-start | bytes 772
  69.9 25.6 %all-to-all-start.1 = ((f32[2,48,2304]{2,0,1:T(2,128)}), f32[2,48,2304]{2,0,1:T(2,128)}, u32[]{:S(2)}, u32[]{:S(2)}) async-start(f32[2,48,2304]{2,0,1:T(2,128)} %copy.22), calls=%async_computation.1 | async-start | bytes 1769472 | tf_op jit(solution)/shard_map/all_to_all | solution.py:247
  74.9 22.6 %collective-permute-start.1 = (f32[1,6,2304]{2,0,1:T(1,128)}, f32[1,6,2304]{2,0,1:T(1,128)}, u32[]{:S(2)}, u32[]{:S(2)}) collective-permute-start(f32[1,6,2304]{2,0,1:T(1,128)} %get-tuple-element.6), channel_id=1, source_target_pairs={{8,0},{16,8},{24,16},{9,1},{17,9},{25,17},{10,2},{18,10},{26,18},{... | collective-permute-start | bytes 165896 | tf_op jit(solution)/shard_map/ppermute | solution.py:233
  76.2 21.3 %collective-permute-start = (f32[1,6,2304]{2,0,1:T(1,128)}, f32[1,6,2304]{2,0,1:T(1,128)}, u32[]{:S(2)}, u32[]{:S(2)}) collective-permute-start(f32[1,6,2304]{2,0,1:T(1,128)} %get-tuple-element.5), channel_id=1, source_target_pairs={{0,8},{8,16},{16,24},{1,9},{9,17},{17,25},{2,10},{10,18},{18,26},{... | collective-permute-start | bytes 165896 | tf_op jit(solution)/shard_map/ppermute | solution.py:231
  89.0 8.5 %copy-start.6 = (f32[16,6,2304]{2,0,1:T(8,128)S(1)}, f32[16,6,2304]{2,0,1:T(8,128)}, u32[]{:S(2)}) copy-start(f32[16,6,2304]{2,0,1:T(8,128)} %reshape.31) | copy-start | bytes 2654212

commit v3 on v2

--- a/solution.py
+++ b/solution.py
@@ -17,7 +17,7 @@
 SCALE = math.sqrt(1.0 + GOLDEN * GOLDEN)
 HALF = 64
 LANES = 128
-BATCH = 4
+BATCH = 8
 BF = jnp.bfloat16
 
 

time: 100 us -> 96.4 us (0.964)
  Pallas kernels: 29.4 us -> 25.5 us
    pallas_call x1, Pallas kernels: 29.4 us -> 25.5 us  [collide(): pl.pallas_call(collide_kernel, out_shape=jax.ShapeDtypeStruct(cells.shape...]
  transfers between devices with their start and end apart: 3 -> 3, of which waited for: 1 -> 1; matrix products, arithmetic and copies ran while one was open for 11% -> 12% of each run, Pallas kernels for 0% -> 0%
where the time goes in v3:
time: 96.4 us; the launch traced here: 95.9 us
  blocking collectives  36 us (37%)
  Pallas kernels  25.5 us (26%)
  local copies, waits for them, and re-layouts  15.5 us (16%)
  starting transfers between devices  9.15 us (9%)
  waiting for transfers between devices  6.59 us (7%)
  other arithmetic  3.08 us (3%)
    all_to_all x1, blocking collectives, body(): lax.all_to_all(distribution, 'vel', split_axis=0, concat_axis=1, tiled=True)  36 us
    pallas_call x1, Pallas kernels, collide(): pl.pallas_call(collide_kernel, out_shape=jax.ShapeDtypeStruct(cells.shape...  25.5 us
    all_to_all x1, waiting for transfers between devices, body(): lax.all_to_all(cell_terms, 'vel', split_axis=1, concat_axis=0, tiled=True)  6.59 us
    reshape x2, local copies, waits for them, and re-layouts, body(): distribution.reshape(cell_count, planes_dev, points, points)[:, :, ::-1, :]  4.81 us
    all_to_all x1, starting transfers between devices, body(): lax.all_to_all(cell_terms, 'vel', split_axis=1, concat_axis=0, tiled=True)  4.22 us
    ppermute x1, starting transfers between devices, padded_2(): lax.ppermute(tail, axis, [(i, (i + 1) % count) for i in range(ends)])  3.65 us
    rev x1, local copies, waits for them, and re-layouts, body(): distribution.reshape(cell_count, planes_dev, points, points)[:, :, ::-1, :]  3.49 us
    unnamed x17, local copies, waits for them, and re-layouts  2.37 us
  transfers between devices with their start and end apart: 3, of which 1 were waited for; matrix products, arithmetic and copies ran while one was open for 12% of the time, Pallas kernels for 0%

profile of v3, /device:TPU:0, one launch (start us, length us, event | category | flops | bytes accessed | tf_op | source)
XLA Modules:
  0.0 95.9 jit_solution(15042216819428661249)
XLA Ops:
  0.0 1.7 %copy.19 = f32[16,6,2304]{2,1,0:T(8,128)S(1)} copy(f32[16,6,2304]{2,0,1:T(8,128)} %param.9) | data formatting | bytes 1769472 | tf_op args[0]
  1.7 36.0 %all_to_all.36 = f32[16,6,2304]{2,1,0:T(8,128)S(1)} all-to-all(f32[16,6,2304]{2,1,0:T(8,128)S(1)} %copy.19), channel_id=1, replica_groups=mesh['space'=4,'vel'=8] {'vel'}, dimensions={0} | all-to-all | bytes 1769472 | tf_op jit(solution)/shard_map/all_to_all | solution.py:243
  37.7 0.0 copy-start
  37.7 0.0 copy-start.1
  37.7 0.0 copy-start.2
  37.7 0.0 copy-start.3
  37.7 0.0 copy-start.4
  37.7 0.5 copy.20
  38.2 0.1 copy.21.u_in
  38.3 0.4 copy-done
  38.7 0.1 copy-done.1
  38.7 0.1 copy-done.2
  38.8 0.1 copy-done.3
  38.9 0.0 copy-done.4
  38.9 25.5 %shard_map.91 = f32[2,48,2304]{2,1,0:T(8,128)S(1)} custom-call(f32[2,48,2304]{2,1,0:T(8,128)S(1)} %copy.21.u_in, f32[6,48,48,128]{3,2,1,0:T(8,128)} %constant.46.clone.spec_hbm, bf16[7,48,144]{2,1,0:T(8,128)(2,1)S(1)} %copy-done.3, bf16[96,144]{1,0:T(8,128)(2,1)S(1)} %copy-done.4, bf16[384,384]{1,0:T(8,128)(2,1)S(1)} %copy-done, ...), custom_call_target="tpu_custom_call" | custom-call | flops 1000000000 | bytes 10485760 | tf_op jit(solution)/shard_map/pallas_call | solution.py:201
  64.4 0.0 copy-start.5
  64.4 0.0 copy-start.7
  64.4 1.6 %copy.22 = f32[2,48,2304]{2,0,1:T(2,128)} copy(f32[2,48,2304]{2,1,0:T(8,128)S(1)} %shard_map.91) | data formatting | bytes 1769472 | tf_op jit(solution)/shard_map/pallas_call | solution.py:201
  66.0 4.2 %all-to-all-start.1 = ((f32[2,48,2304]{2,0,1:T(2,128)}), f32[2,48,2304]{2,0,1:T(2,128)}, u32[]{:S(2)}, u32[]{:S(2)}) async-start(f32[2,48,2304]{2,0,1:T(2,128)} %copy.22), calls=%async_computation.1 | async-start | bytes 1769472 | tf_op jit(solution)/shard_map/all_to_all | solution.py:247
  70.3 0.0 copy-done.5
  70.3 0.7 fusion.16
  71.0 1.3 %collective-permute-start.1 = (f32[1,6,2304]{2,0,1:T(1,128)}, f32[1,6,2304]{2,0,1:T(1,128)}, u32[]{:S(2)}, u32[]{:S(2)}) collective-permute-start(f32[1,6,2304]{2,0,1:T(1,128)} %get-tuple-element.6), channel_id=1, source_target_pairs={{8,0},{16,8},{24,16},{9,1},{17,9},{25,17},{10,2},{18,10},{26,18},{... | collective-permute-start | bytes 165896 | tf_op jit(solution)/shard_map/ppermute | solution.py:233
  72.3 3.7 %collective-permute-start = (f32[1,6,2304]{2,0,1:T(1,128)}, f32[1,6,2304]{2,0,1:T(1,128)}, u32[]{:S(2)}, u32[]{:S(2)}) collective-permute-start(f32[1,6,2304]{2,0,1:T(1,128)} %get-tuple-element.5), channel_id=1, source_target_pairs={{0,8},{8,16},{16,24},{1,9},{9,17},{17,25},{2,10},{10,18},{18,26},{... | collective-permute-start | bytes 165896 | tf_op jit(solution)/shard_map/ppermute | solution.py:231
  75.9 0.0 copy-done.7
  75.9 0.1 pad_add_fusion
  76.0 0.1 dynamic_slice.3
  76.1 0.7 slice_compare_fusion.1
  76.8 2.9 %reshape.30 = f32[16,6,48,48]{3,2,0,1:T(8,128)} reshape(f32[16,6,2304]{2,0,1:T(8,128)S(1)} %copy-done.5) | data formatting | bytes 1769472 | tf_op jit(solution)/shard_map/reshape | solution.py:250
  79.6 3.5 %rev.3 = f32[16,6,48,48]{3,2,0,1:T(8,128)S(1)} reverse(f32[16,6,48,48]{3,2,0,1:T(8,128)} %reshape.30), dimensions={2} | reverse | bytes 1769472 | tf_op jit(solution)/shard_map/rev | solution.py:250
  83.1 1.9 %reshape.31 = f32[16,6,2304]{2,0,1:T(8,128)} reshape(f32[16,6,48,48]{3,2,0,1:T(8,128)S(1)} %rev.3) | data formatting | bytes 1769472 | tf_op jit(solution)/shard_map/reshape | solution.py:250
  85.1 0.0 copy-start.6
  85.1 6.6 %all-to-all-done.1 = f32[2,48,2304]{2,0,1:T(2,128)} async-done(((f32[2,48,2304]{2,0,1:T(2,128)}), f32[2,48,2304]{2,0,1:T(2,128)}, u32[]{:S(2)}, u32[]{:S(2)}) %all-to-all-start.1) | async-done | bytes 884768 | tf_op jit(solution)/shard_map/all_to_all | solution.py:247
  91.7 1.3 %copy.23 = f32[8,2,6,2304]{3,1,0,2:T(2,128)S(1)} copy(f32[8,2,6,2304]{3,1,2,0:T(2,128)} %bitcast.4) | data formatting | bytes 1769472 | tf_op jit(solution)/shard_map/all_to_all | solution.py:247
  92.9 0.6 all_to_all.33
  93.5 0.0 collective-permute-done.1
  93.5 0.0 collective-permute-done
  93.6 0.0 copy-done.6
  93.6 2.3 %fusion.5 = f32[16,6,2304]{2,0,1:T(8,128)} fusion(f32[16,6,2304]{2,0,1:T(8,128)S(1)} %copy-done.5, f32[16,6,2304]{2,0,1:T(8,128)S(1)} %copy-done.6, f32[1,6,2304]{2,0,1:T(1,128)} %collective-permute-done.1, f32[1,6,2304]{2,0,1:T(1,128)} %collective-permute-done, f32[16,6,2304]{2,0,1:T(8,128)S(1)} %all_to_all.33, f32[16]{0:T(128)} %param.10, ...), kind=kLoop, calls=%fused_computation.6 | loop fusion | flops 2875392 | bytes 3661168 | tf_op jit(solution)/shard_map/add | solution.py:266
  (2 shorter events, 0.0 us)
Async XLA Ops:
  37.7 1.0 %copy-start = (bf16[384,384]{1,0:T(8,128)(2,1)S(1)}, bf16[384,384]{1,0:T(8,128)(2,1)}, u32[]{:S(2)}) copy-start(bf16[384,384]{1,0:T(8,128)(2,1)} %constant.49.clone.rf) | copy-start | bytes 884740
  37.7 1.0 %copy-start.1 = (bf16[2,384,128]{2,1,0:T(8,128)(2,1)S(1)}, bf16[2,384,128]{2,1,0:T(8,128)(2,1)}, u32[]{:S(2)}) copy-start(bf16[2,384,128]{2,1,0:T(8,128)(2,1)} %constant.50.clone.rr) | copy-start | bytes 589828
  37.7 1.1 %copy-start.2 = (bf16[384,256]{1,0:T(8,128)(2,1)S(1)}, bf16[384,256]{1,0:T(8,128)(2,1)}, u32[]{:S(2)}) copy-start(bf16[384,256]{1,0:T(8,128)(2,1)} %constant.51.clone.rg) | copy-start | bytes 589828
  37.7 1.2 %copy-start.3 = (bf16[7,48,144]{2,1,0:T(8,128)(2,1)S(1)}, bf16[7,48,144]{2,1,0:T(8,128)(2,1)}, u32[]{:S(2)}) copy-start(bf16[7,48,144]{2,1,0:T(8,128)(2,1)} %constant.47.clone.la) | copy-start | bytes 290308
  37.7 1.2 %copy-start.4 = (bf16[96,144]{1,0:T(8,128)(2,1)S(1)}, bf16[96,144]{1,0:T(8,128)(2,1)}, u32[]{:S(2)}) copy-start(bf16[96,144]{1,0:T(8,128)(2,1)} %constant.48.clone.lp) | copy-start | bytes 82948
  64.4 5.9 %copy-start.5 = (f32[16,6,2304]{2,0,1:T(8,128)S(1)}, f32[16,6,2304]{2,0,1:T(8,128)}, u32[]{:S(2)}) copy-start(f32[16,6,2304]{2,0,1:T(8,128)} %param.9) | copy-start | bytes 2654212
  64.4 11.5 %copy-start.7 = (s32[64]{0:T(128)S(1)}, s32[64]{0:T(128)}, u32[]{:S(2)}) copy-start(s32[64]{0:T(128)} %param.11) | copy-start | bytes 772
  66.0 25.6 %all-to-all-start.1 = ((f32[2,48,2304]{2,0,1:T(2,128)}), f32[2,48,2304]{2,0,1:T(2,128)}, u32[]{:S(2)}, u32[]{:S(2)}) async-start(f32[2,48,2304]{2,0,1:T(2,128)} %copy.22), calls=%async_computation.1 | async-start | bytes 1769472 | tf_op jit(solution)/shard_map/all_to_all | solution.py:247
  71.0 22.6 %collective-permute-start.1 = (f32[1,6,2304]{2,0,1:T(1,128)}, f32[1,6,2304]{2,0,1:T(1,128)}, u32[]{:S(2)}, u32[]{:S(2)}) collective-permute-start(f32[1,6,2304]{2,0,1:T(1,128)} %get-tuple-element.6), channel_id=1, source_target_pairs={{8,0},{16,8},{24,16},{9,1},{17,9},{25,17},{10,2},{18,10},{26,18},{... | collective-permute-start | bytes 165896 | tf_op jit(solution)/shard_map/ppermute | solution.py:233
  72.3 21.3 %collective-permute-start = (f32[1,6,2304]{2,0,1:T(1,128)}, f32[1,6,2304]{2,0,1:T(1,128)}, u32[]{:S(2)}, u32[]{:S(2)}) collective-permute-start(f32[1,6,2304]{2,0,1:T(1,128)} %get-tuple-element.5), channel_id=1, source_target_pairs={{0,8},{8,16},{16,24},{1,9},{9,17},{17,25},{2,10},{10,18},{18,26},{... | collective-permute-start | bytes 165896 | tf_op jit(solution)/shard_map/ppermute | solution.py:231
  85.1 8.5 %copy-start.6 = (f32[16,6,2304]{2,0,1:T(8,128)S(1)}, f32[16,6,2304]{2,0,1:T(8,128)}, u32[]{:S(2)}) copy-start(f32[16,6,2304]{2,0,1:T(8,128)} %reshape.31) | copy-start | bytes 2654212
